TPU v7x, 256 devices: a whole 4x4x8 slice. The times are simulated.
256 devices in a mesh: tm: 16 (over z_lo, x, core), space: 16 (over z_hi, y).
Axes of the slice: x: 4, y: 4, z: 8 (z_hi: 4, z_lo: 2; z = z_hi * 2 + z_lo), core: 2. Of those that a mesh axis runs over, the one named last changes fastest.
Arguments:
- tokens: bfloat16 [1680, 64, 256], P('space', 'tm'), may hold values from -11 to 11
- w_query: bfloat16 [256, 256], replicated, may hold values from -0.375 to 0.375
- w_key: bfloat16 [256, 256], replicated, may hold values from -0.375 to 0.375
- w_value: bfloat16 [256, 256], replicated, may hold values from -0.375 to 0.375
- w_out: bfloat16 [256, 256], replicated, may hold values from -0.375 to 0.375
- mask: int32 [1680, 1680], P('space'), may hold values from 0 to 1, as said below
- decay: float32 [64, 256], P('tm'), may hold values from 0 to 1
- cotangent: float32 [1680, 64, 256], P('space', 'tm'), may hold values from -6 to 6
Outputs:
- grad_tokens: float32 [1680, 64, 256], P('space', 'tm')
- grad_wq: float32 [256, 256], replicated
- grad_wk: float32 [256, 256], replicated
- grad_wv: float32 [256, 256], replicated
- output_weight_gradient: float32 [256, 256], replicated
Inputs may be any that keep to these rules, and one draw needn't show every extreme that they name: `mask`: every token may attend to itself.
All inputs are finite; a program needn't handle non-finite values.
Results may differ from a plain program's by a relative error of at most 0.03.
The roundings to bfloat16 on the way count: a program that leaves them out, or rounds other values in their place, can miss the bound.
Values may be sent and summed in bfloat16 or wider, within the bound.
A program may use at most 128 MiB of HBM per device.

v0:
```python
import math
import jax
import jax.numpy as jnp
from jax import lax
from jax.sharding import PartitionSpec as P

HEADS = 8


def shifted(array, axis, by):
    devices = lax.axis_size(axis)
    pairs = [(i, i + by) for i in range(devices) if 0 <= i + by < devices]
    return lax.ppermute(array, axis, pairs)


def project(rows_flat, weight):
    return jnp.dot(rows_flat, weight, preferred_element_type=jnp.float32).astype(jnp.bfloat16)


def cross(left, right):
    return lax.dot_general(
        left, right, (((0,), (0,)), ((), ())), preferred_element_type=jnp.float32
    )


def back_project(grads_b, weight):
    return lax.dot_general(
        grads_b, weight, (((1,), (1,)), ((), ())), preferred_element_type=jnp.float32
    )


def shards(tokens, w_query, w_key, w_value, w_out, mask, decay, cotangent):
    tok_rows, round_rows, features = tokens.shape
    head_size = features // HEADS
    score_scale = 1.0 / math.sqrt(head_size)
    x_rounds = jnp.swapaxes(tokens, 0, 1)
    flat_rows = x_rounds.reshape(-1, features)
    queries = project(flat_rows, w_query).reshape(round_rows, tok_rows, HEADS, head_size)
    own_keys = project(flat_rows, w_key).reshape(round_rows, tok_rows, features)
    own_values = project(flat_rows, w_value).reshape(round_rows, tok_rows, features)
    all_keys, all_values = (
        lax.all_gather(own_keys, "space", axis=1, tiled=True),
        lax.all_gather(own_values, "space", axis=1, tiled=True),
    )
    random_key_count = all_keys.shape[1]
    all_keys = all_keys.reshape(round_rows, random_key_count, HEADS, head_size)
    all_values = all_values.reshape(round_rows, random_key_count, HEADS, head_size)
    allowed = mask > 0

    def masked_scores(q_round, k_round):
        scores = (
            jnp.einsum("ihe,jhe->hij", q_round, k_round, preferred_element_type=jnp.float32)
            * score_scale
        )
        return jnp.where(allowed[None], scores, -1e30)

    def forward(round_index):
        scores = masked_scores(queries[round_index], all_keys[round_index])
        maxima = jnp.max(scores, axis=2, keepdims=True)
        expons = jnp.exp(scores - maxima)
        totals = jnp.sum(expons, axis=2, keepdims=True)
        probs_b = (expons / totals).astype(jnp.bfloat16)
        stack_result_matrix = jnp.einsum(
            "hij,jhe->ihe", probs_b, all_values[round_index], preferred_element_type=jnp.float32
        )
        return (stack_result_matrix.astype(jnp.bfloat16), maxima, totals)

    attended, maxima, totals = lax.map(forward, jnp.arange(round_rows))
    local_grads = [None] * round_rows
    reach = [None] * round_rows
    local_grads[round_rows - 1] = cotangent[:, round_rows - 1]
    reach[round_rows - 1] = jnp.ones((1, features), jnp.float32)
    for position in range(round_rows - 2, -1, -1):
        local_grads[position] = (
            cotangent[:, position] + decay[position + 1][None] * local_grads[position + 1]
        )
        reach[position] = decay[position + 1][None] * reach[position + 1]
    block_decay = decay[0][None] * reach[0]
    block_update_message = decay[0][None] * local_grads[0]

    def relay(step_index, state):
        incoming, message = state
        incoming = shifted(message.astype(jnp.bfloat16), "tm", -1).astype(message.dtype)
        return (incoming, block_update_message + block_decay * incoming)

    carried, unused = lax.fori_loop(
        0, lax.axis_size("tm"), relay, (jnp.zeros_like(block_update_message), block_update_message)
    )
    grads = jnp.stack(
        [local_grads[position] + reach[position] * carried for position in range(round_rows)],
        axis=0,
    )
    grads_flat = grads.astype(jnp.bfloat16).reshape(-1, features)
    attended_flat = attended.reshape(-1, features)
    output_weight_gradient = cross(attended_flat, grads_flat)
    upstream = (
        back_project(grads_flat, w_out)
        .astype(jnp.bfloat16)
        .reshape(round_rows, tok_rows, HEADS, head_size)
    )
    deltas = jnp.sum(upstream.astype(jnp.float32) * attended.astype(jnp.float32), axis=3)
    deltas = jnp.swapaxes(deltas, 1, 2)[..., None]

    def backward_round(round_index):
        k_round = all_keys[round_index]
        v_round = all_values[round_index]
        q_round = queries[round_index]
        up_round = upstream[round_index]
        scores = masked_scores(q_round, k_round)
        probs = jnp.exp(scores - maxima[round_index]) / totals[round_index]
        slopes = jnp.einsum("ihe,jhe->hij", up_round, v_round, preferred_element_type=jnp.float32)
        score_grads = (probs * (slopes - deltas[round_index])).astype(jnp.bfloat16)
        grad_query = (
            jnp.einsum("hij,jhe->ihe", score_grads, k_round, preferred_element_type=jnp.float32)
            * score_scale
        )
        grad_key = (
            jnp.einsum("hij,ihe->jhe", score_grads, q_round, preferred_element_type=jnp.float32)
            * score_scale
        )
        grad_value = jnp.einsum(
            "hij,ihe->jhe", probs.astype(jnp.bfloat16), up_round, preferred_element_type=jnp.float32
        )
        partials = jnp.concatenate(
            [
                grad_key.reshape(random_key_count, features),
                grad_value.reshape(random_key_count, features),
            ],
            axis=1,
        )
        partials = partials.astype(jnp.bfloat16).astype(jnp.float32)
        return (grad_query.astype(jnp.bfloat16), partials)

    grad_queries, partial_terms = lax.map(backward_round, jnp.arange(round_rows))
    partial_terms = jnp.swapaxes(partial_terms, 0, 1)
    kv_grads = lax.psum_scatter(
        partial_terms.astype(jnp.bfloat16), "space", scatter_dimension=0, tiled=True
    ).astype(jnp.float32)
    kv_grads = jnp.swapaxes(kv_grads, 0, 1)
    grad_keys = kv_grads[..., :features].astype(jnp.bfloat16).reshape(-1, features)
    grad_values = kv_grads[..., features:].astype(jnp.bfloat16).reshape(-1, features)
    grad_q_flat = grad_queries.reshape(-1, features)
    grad_rows = grads.reshape(-1, features) + back_project(grad_q_flat, w_query)
    grad_rows = grad_rows + back_project(grad_keys, w_key) + back_project(grad_values, w_value)
    grad_tokens = jnp.swapaxes(grad_rows.reshape(round_rows, tok_rows, features), 0, 1)
    summed = lax.psum(
        (
            cross(flat_rows, grad_q_flat),
            cross(flat_rows, grad_keys),
            cross(flat_rows, grad_values),
            output_weight_gradient,
        ),
        ("tm", "space"),
    )
    return (grad_tokens, summed[0], summed[1], summed[2], summed[3])


def solution(mesh):
    return jax.shard_map(
        shards,
        mesh=mesh,
        in_specs=(
            P("space", "tm", None),
            P(),
            P(),
            P(),
            P(),
            P("space", None),
            P("tm", None),
            P("space", "tm", None),
        ),
        out_specs=(P("space", "tm", None), P(), P(), P(), P()),
        check_vma=False,
    )
```

profile of v0, /device:TPU:8, one launch (start us, length us, event | category | flops | bytes accessed | tf_op | source)
XLA Modules:
  0.0 1136.6 jit_solution(881701952524546462)
XLA Ops:
  14.5 117.5 %while.38 = (s32[]{:T(128)}, f32[105,256]{1,0:T(8,128)}, bf16[105,256]{1,0:T(8,128)(2,1)S(1)}, f32[1,256]{1,0:T(1,128)S(1)}, f32[105,256]{1,0:T(8,128)S(1)}, /*index=5*/s32[]{:T(128)}) while((s32[]{:T(128)}, f32[105,256]{1,0:T(8,128)}, bf16[105,256]{1,0:T(8,128)(2,1)S(1)}, f32[1,256]{1,0:T(1,128)S(1)}, f32[105,256]{1,0:T(8,128)S(1)}, ...), condition=%wide.region_1.2_spmd, body=%wide.region_0.1_spmd.sunk | while | flops 107522 | bytes 538733 | solution.py:86
  14.5 1.3 collective-permute-start
  15.8 1.8 collective-permute-done
  18.3 1.3 collective-permute-start
  19.6 3.6 collective-permute-done
  23.9 1.3 collective-permute-start
  25.1 4.2 collective-permute-done
  30.0 1.3 collective-permute-start
  31.3 4.6 collective-permute-done
  37.8 4.6 collective-permute-done
  44.4 4.2 collective-permute-done
  50.5 4.2 collective-permute-done
  56.7 4.6 collective-permute-done
  63.2 4.6 collective-permute-done
  69.8 4.6 collective-permute-done
  76.3 5.4 collective-permute-done
  83.7 10.1 collective-permute-done
  95.7 10.1 collective-permute-done
  107.8 7.1 collective-permute-done
  116.8 6.3 collective-permute-done
  125.1 6.3 collective-permute-done
  134.7 6.9 copy.82
  141.5 12.3 %all-gather.5.cloned.1.call-done = bf16[4,1680,256]{2,0,1:T(4,128)(2,1)} async-done(((bf16[4,105,256]{2,0,1:T(4,128)(2,1)}), bf16[4,1680,256]{2,0,1:T(4,128)(2,1)}) %all-gather.5.cloned.1.call-update) | async-done | bytes 3440656 | tf_op jit(solution)/shard_map/all_gather | solution.py:43
  153.8 6.9 copy.85
  160.8 39.1 %while.39 = (s32[]{:T(128)}, bf16[4,105,8,32]{1,3,2,0:T(8,128)(2,1)S(1)}, f32[4,8,105,1]{2,1,3,0:T(8,128)S(1)}, f32[4,8,105,1]{2,1,3,0:T(8,128)S(1)}, s32[4]{0:T...) while((s32[]{:T(128)}, ...), condition=%wide.region_5.6_spmd, body=%wide.region_2.5_spmd.sunk | while | flops 197593216 | bytes 20291880 | solution.py:68
  163.3 2.6 fusion.96
  165.9 1.6 fusion.97
  167.5 3.0 fusion.98
  173.1 2.6 fusion.96
  175.7 1.6 fusion.97
  177.3 3.0 fusion.98
  182.9 2.6 fusion.96
  185.5 1.6 fusion.97
  187.1 3.0 fusion.98
  192.6 2.6 fusion.96
  195.2 1.6 fusion.97
  196.9 3.0 fusion.98
  200.2 316.6 %while.40 = (s32[]{:T(128)}, bf16[4,105,8,32]{1,3,2,0:T(8,128)(2,1)S(1)}, bf16[4,1680,512]{2,0,1:T(4,128)(2,1)}, s32[4]{0:T(128)S(1)}, bf16[4,1680,8,32]{1,3,2,0...) while((s32[]{:T(128)}, ...), condition=%wide.region_8.9_spmd, body=%wide.region_7.8_spmd.sunk | while | flops 467658240 | bytes 43092636 | solution.py:134
  202.8 3.4 exponential_divide_fusion.2
  206.7 2.3 multiply_convert_fusion.2
  209.0 2.3 fusion.109
  212.0 6.3 copy.148
  218.4 61.0 %dynamic_update_slice.29 = bf16[4,1680,512]{2,0,1:T(4,128)(2,1)} dynamic-update-slice(bf16[4,1680,512]{2,0,1:T(4,128)(2,1)} %get-tuple-element.583, bf16[1,1680,512]{2,0,1:T(2,128)(2,1)} %copy.148, s32[]{:T(128)S(6)} %copy.178, s32[]{:T(128)} %constant.35.clone.1..sunk.1, s32[]{:T(128)} %constant.35.clone.1..sunk.1) | dynamic-update-slice | bytes 3440644 | tf_op jit(solution)/shard_map/while/body/jit(dynamic_update_index_in_dim)/dynamic_update_slice | solution.py:134
  281.9 3.4 exponential_divide_fusion.2
  285.9 2.3 multiply_convert_fusion.2
  288.1 2.3 fusion.109
  291.2 6.3 copy.148
  297.5 61.0 %dynamic_update_slice.29 = bf16[4,1680,512]{2,0,1:T(4,128)(2,1)} dynamic-update-slice(bf16[4,1680,512]{2,0,1:T(4,128)(2,1)} %get-tuple-element.583, bf16[1,1680,512]{2,0,1:T(2,128)(2,1)} %copy.148, s32[]{:T(128)S(6)} %copy.178, s32[]{:T(128)} %constant.35.clone.1..sunk.1, s32[]{:T(128)} %constant.35.clone.1..sunk.1) | dynamic-update-slice | bytes 3440644 | tf_op jit(solution)/shard_map/while/body/jit(dynamic_update_index_in_dim)/dynamic_update_slice | solution.py:134
  361.0 3.4 exponential_divide_fusion.2
  365.0 2.3 multiply_convert_fusion.2
  367.3 2.3 fusion.109
  370.3 6.3 copy.148
  376.7 61.0 %dynamic_update_slice.29 = bf16[4,1680,512]{2,0,1:T(4,128)(2,1)} dynamic-update-slice(bf16[4,1680,512]{2,0,1:T(4,128)(2,1)} %get-tuple-element.583, bf16[1,1680,512]{2,0,1:T(2,128)(2,1)} %copy.148, s32[]{:T(128)S(6)} %copy.178, s32[]{:T(128)} %constant.35.clone.1..sunk.1, s32[]{:T(128)} %constant.35.clone.1..sunk.1) | dynamic-update-slice | bytes 3440644 | tf_op jit(solution)/shard_map/while/body/jit(dynamic_update_index_in_dim)/dynamic_update_slice | solution.py:134
  440.2 3.4 exponential_divide_fusion.2
  444.1 2.3 multiply_convert_fusion.2
  446.4 2.3 fusion.109
  449.5 6.3 copy.148
  455.8 61.0 %dynamic_update_slice.29 = bf16[4,1680,512]{2,0,1:T(4,128)(2,1)} dynamic-update-slice(bf16[4,1680,512]{2,0,1:T(4,128)(2,1)} %get-tuple-element.583, bf16[1,1680,512]{2,0,1:T(2,128)(2,1)} %copy.148, s32[]{:T(128)S(6)} %copy.178, s32[]{:T(128)} %constant.35.clone.1..sunk.1, s32[]{:T(128)} %constant.35.clone.1..sunk.1) | dynamic-update-slice | bytes 3440644 | tf_op jit(solution)/shard_map/while/body/jit(dynamic_update_index_in_dim)/dynamic_update_slice | solution.py:134
  522.2 331.0 %all-reduce.5.cloned.1.call-done = bf16[1680,4,512]{2,1,0:T(4,128)(2,1)} async-done(((bf16[1680,4,512]{2,1,0:T(4,128)(2,1)}), bf16[1680,4,512]{2,1,0:T(4,128)(2,1)}) %all-reduce.5.cloned.1.call-update) | async-done | bytes 6881296
  858.3 264.8 %all-reduce.7.cloned.1.call-done = (f32[256,256]{0,1:T(8,128)}, f32[256,256]{0,1:T(8,128)}, f32[256,256]{0,1:T(8,128)}, f32[256,256]{1,0:T(8,128)}) async-done(((f32[256,256]{0,1:T(8,128)}, f32[256,256]{0,1:T(8,128)}, f32[256,256]{0,1:T(8,128)}, f32[256,256]{1,0:T(8,128)}), (f32[256,256]{0,1:T(8,128)}, f32[256,256]{0,1:T(8,128)}, f32[256,256]{0,1:T(8,128)}, ...) | async-done | bytes 1048592 | tf_op jit(solution)/shard_map/psum | solution.py:146
  1123.0 1.8 copy.99
  1124.8 1.8 copy.100
  1126.6 1.8 copy.101
  1128.4 1.7 copy.189
  (162 shorter events, 55.3 us)
Async XLA Ops:
  7.2 5.5 copy-start
  7.2 7.0 copy-start.16
  7.2 126.6 %copy-start.18 = (bf16[256,256]{1,0:T(8,128)(2,1)S(1)}, bf16[256,256]{1,0:T(8,128)(2,1)}, u32[]{:S(2)}) copy-start(bf16[256,256]{1,0:T(8,128)(2,1)} %param.18) | copy-start | bytes 393220
  7.2 127.5 %all-gather.3.cloned.1.call-start = ((), (), s32[]{:S(2)}) async-start(), calls=%async_computation | async-start | bytes 3655680 | tf_op jit(solution)/shard_map/all_gather | solution.py:42
  8.3 125.9 %copy-start.1 = (bf16[420,256]{1,0:T(8,128)(2,1)}, bf16[420,256]{1,0:T(8,128)(2,1)S(1)}, u32[]{:S(2)}) copy-start(bf16[420,256]{1,0:T(8,128)(2,1)S(1)} %reshape.106) | copy-start | bytes 645124
  10.4 124.1 %copy-start.13 = (s32[105,1680]{1,0:T(8,128)S(1)}, s32[105,1680]{1,0:T(8,128)}, u32[]{:S(2)}) copy-start(s32[105,1680]{1,0:T(8,128)} %param.19) | copy-start | bytes 2116804
  10.5 143.4 %all-gather.5.cloned.1.call-start = ((), (), s32[]{:S(2)}) async-start(), calls=%async_computation.1 | async-start | bytes 3655680 | tf_op jit(solution)/shard_map/all_gather | solution.py:43
  12.6 840.6 %all-reduce.5.cloned.1.call-start = ((), (), s32[]{:S(2)}) async-start(), calls=%async_computation.2 | async-start | bytes 13762560
  14.5 3.1 collective-permute-start
  18.3 4.9 collective-permute-start
  23.9 5.5 collective-permute-start
  30.0 5.9 collective-permute-start
  36.5 5.9 collective-permute-start
  43.1 5.5 collective-permute-start
  49.2 5.5 collective-permute-start
  55.4 5.9 collective-permute-start
  61.9 5.9 collective-permute-start
  68.5 5.9 collective-permute-start
  75.0 6.7 collective-permute-start
  82.4 11.3 collective-permute-start
  94.4 11.4 %collective-permute-start = (bf16[105,256]{1,0:T(8,128)(2,1)S(1)}, bf16[105,256]{1,0:T(8,128)(2,1)S(1)}, u32[]{:S(2)}, u32[]{:S(2)}) collective-permute-start(bf16[105,256]{1,0:T(8,128)(2,1)S(1)} %get-tuple-element.520), channel_id=1, source_target_pairs={{16,0},{32,16},{48,32},{64,48},{80,64},{96,80},{112,96},{128,112},... | collective-permute-start | bytes 161288 | tf_op jit(solution)/shard_map/while/body/eval_jaxpr/ppermute | solution.py:13
  106.5 8.4 collective-permute-start
  115.5 7.6 collective-permute-start
  123.8 7.6 collective-permute-start
  133.0 0.7 copy-start.7
  133.0 0.7 copy-start.9
  133.0 0.7 copy-start.11
  133.0 1.4 copy-start.5
  133.8 26.9 %copy-start.3 = (f32[420,256]{1,0:T(8,128)}, f32[420,256]{1,0:T(8,128)S(1)}, u32[]{:S(2)}) copy-start(f32[420,256]{1,0:T(8,128)S(1)} %reshape.105) | copy-start | bytes 1290244
  516.8 0.9 copy-start.6
  516.8 1.0 copy-start.8
  516.8 1.0 copy-start.10
  516.8 1.1 copy-start.12
  516.8 1.2 copy-start.19
  516.8 3.2 copy-start.2
  516.8 5.1 copy-start.4
  516.8 337.7 %copy-start.17 = (bf16[105,4,256]{2,1,0:T(4,128)(2,1)S(1)}, bf16[105,4,256]{2,1,0:T(4,128)(2,1)}, u32[]{:S(2)}) copy-start(bf16[105,4,256]{2,1,0:T(4,128)(2,1)} %param.14) | copy-start | bytes 645124
  516.9 339.8 %copy-start.14 = (bf16[256,256]{1,0:T(8,128)(2,1)S(1)}, bf16[256,256]{1,0:T(8,128)(2,1)}, u32[]{:S(2)}) copy-start(bf16[256,256]{1,0:T(8,128)(2,1)} %param.16) | copy-start | bytes 393220
  516.9 606.2 %all-reduce.7.cloned.1.call-start = ((), (), s32[]{:S(2)}) async-start(), calls=%async_computation.3 | async-start | bytes 2097152 | tf_op jit(solution)/shard_map/psum | solution.py:146
  517.9 339.0 %copy-start.15 = (bf16[256,256]{1,0:T(8,128)(2,1)S(1)}, bf16[256,256]{1,0:T(8,128)(2,1)}, u32[]{:S(2)}) copy-start(bf16[256,256]{1,0:T(8,128)(2,1)} %param.17) | copy-start | bytes 393220
Sparse Core Ops, SparseCore 0:
  11.0 71.6 all-gather.2
  85.7 68.0 all-gather.4
  517.0 336.1 all-reduce.4
  860.4 262.5 all-reduce.6
where the time goes:
time: 1160 us; the launch traced here: 1140 us
  waiting for transfers between devices  694 us (60%)
  local copies, waits for them, and re-layouts  304 us (26%)
  matrix products  66.1 us (6%)
  starting transfers between devices  20.8 us (2%)
  other arithmetic  20 us (2%)
  loops' own time  16.1 us (1%)
  between operations  15 us (1%)
    unnamed x5, waiting for transfers between devices  331 us
    dynamic_update_slice x8, local copies, waits for them, and re-layouts, shards(): lax.map(backward_round, jnp.arange(round_rows))  269 us
    psum x1, waiting for transfers between devices, shards(): lax.psum((cross(flat_rows, grad_q_flat), cross(flat_rows, grad_keys), cro...  265 us
    ppermute x16, waiting for transfers between devices, shifted(): return lax.ppermute(array, axis, pairs)  86.3 us
    dot_general x8, matrix products, masked_scores(): jnp.einsum('ihe,jhe->hij', q_round, k_round, preferred_element_type=jnp.f...  23.9 us
  transfers between devices with their start and end apart: 20, of which 19 were waited for; matrix products, arithmetic and copies ran while one was open for 3% of the time, Pallas kernels for 0%

commit v1 on v0

--- a/solution.py
+++ b/solution.py
@@ -143,15 +143,14 @@
     grad_rows = grads.reshape(-1, features) + back_project(grad_q_flat, w_query)
     grad_rows = grad_rows + back_project(grad_keys, w_key) + back_project(grad_values, w_value)
     grad_tokens = jnp.swapaxes(grad_rows.reshape(round_rows, tok_rows, features), 0, 1)
-    summed = lax.psum(
-        (
-            cross(flat_rows, grad_q_flat),
-            cross(flat_rows, grad_keys),
-            cross(flat_rows, grad_values),
-            output_weight_gradient,
-        ),
-        ("tm", "space"),
+    summed = (
+        cross(flat_rows, grad_q_flat),
+        cross(flat_rows, grad_keys),
+        cross(flat_rows, grad_values),
+        output_weight_gradient,
     )
+    for over in ("tm", "space"):
+        summed = lax.psum(summed, over)
     return (grad_tokens, summed[0], summed[1], summed[2], summed[3])
 
 

time: 1160 us -> 1190 us (1.026)
  waiting for transfers between devices: 694 us -> 732 us
    psum x1 -> x2, waiting for transfers between devices: 265 us -> 301 us  [shards(): summed = lax.psum(summed, over)]
    unnamed x5 -> x6, waiting for transfers between devices: 331 us -> 332 us
  transfers between devices with their start and end apart: 20 -> 21, of which waited for: 19 -> 20; matrix products, arithmetic and copies ran while one was open for 3% -> 2% of each run, Pallas kernels for 0% -> 0%
where the time goes in v1:
time: 1190 us; the launch traced here: 1170 us
  waiting for transfers between devices  732 us (62%)
  local copies, waits for them, and re-layouts  304 us (26%)
  matrix products  66.4 us (6%)
  starting transfers between devices  20.9 us (2%)
  other arithmetic  20.2 us (2%)
  loops' own time  16.1 us (1%)
  between operations  15 us (1%)
    unnamed x6, waiting for transfers between devices  332 us
    psum x2, waiting for transfers between devices, shards(): summed = lax.psum(summed, over)  301 us
    dynamic_update_slice x8, local copies, waits for them, and re-layouts, shards(): lax.map(backward_round, jnp.arange(round_rows))  269 us
    ppermute x16, waiting for transfers between devices, shifted(): return lax.ppermute(array, axis, pairs)  86.3 us
    dot_general x8, matrix products, masked_scores(): jnp.einsum('ihe,jhe->hij', q_round, k_round, preferred_element_type=jnp.f...  23.9 us
  transfers between devices with their start and end apart: 21, of which 20 were waited for; matrix products, arithmetic and copies ran while one was open for 2% of the time, Pallas kernels for 0%

profile of v1, /device:TPU:8, one launch (start us, length us, event | category | flops | bytes accessed | tf_op | source)
XLA Modules:
  0.0 1173.9 jit_solution(18399996380067718058)
XLA Ops:
  14.5 117.6 %while.38 = (s32[]{:T(128)}, f32[105,256]{1,0:T(8,128)}, bf16[105,256]{1,0:T(8,128)(2,1)S(1)}, f32[1,256]{1,0:T(1,128)S(1)}, f32[105,256]{1,0:T(8,128)S(1)}, /*index=5*/s32[]{:T(128)}) while((s32[]{:T(128)}, f32[105,256]{1,0:T(8,128)}, bf16[105,256]{1,0:T(8,128)(2,1)S(1)}, f32[1,256]{1,0:T(1,128)S(1)}, f32[105,256]{1,0:T(8,128)S(1)}, ...), condition=%wide.region_1.2_spmd, body=%wide.region_0.1_spmd.sunk | while | flops 107522 | bytes 538733 | solution.py:86
  14.5 1.3 collective-permute-start
  15.8 1.8 collective-permute-done
  18.3 1.3 collective-permute-start
  19.6 3.6 collective-permute-done
  23.9 1.3 collective-permute-start
  25.1 4.2 collective-permute-done
  31.3 4.6 collective-permute-done
  37.8 4.6 collective-permute-done
  44.4 4.2 collective-permute-done
  50.5 4.2 collective-permute-done
  56.7 4.6 collective-permute-done
  63.2 4.6 collective-permute-done
  69.8 4.6 collective-permute-done
  76.3 5.4 collective-permute-done
  83.7 10.0 collective-permute-done
  95.7 10.1 collective-permute-done
  107.8 7.1 collective-permute-done
  116.9 6.2 collective-permute-done
  125.0 6.4 collective-permute-done
  134.7 6.9 copy.82
  141.7 12.1 %all-gather.5.cloned.1.call-done = bf16[4,1680,256]{2,0,1:T(4,128)(2,1)} async-done(((bf16[4,105,256]{2,0,1:T(4,128)(2,1)}), bf16[4,1680,256]{2,0,1:T(4,128)(2,1)}) %all-gather.5.cloned.1.call-update) | async-done | bytes 3440656 | tf_op jit(solution)/shard_map/all_gather | solution.py:43
  153.8 6.8 copy.85
  160.7 39.7 %while.39 = (s32[]{:T(128)}, bf16[4,105,8,32]{1,3,2,0:T(8,128)(2,1)S(1)}, f32[4,8,105,1]{2,1,3,0:T(8,128)S(1)}, f32[4,8,105,1]{2,1,3,0:T(8,128)S(1)}, s32[4]{0:T...) while((s32[]{:T(128)}, ...), condition=%wide.region_5.6_spmd, body=%wide.region_2.5_spmd.sunk | while | flops 197593216 | bytes 20291880 | solution.py:68
  163.2 2.6 fusion.96
  165.8 1.7 fusion.97
  167.5 3.1 fusion.98
  173.1 2.6 fusion.96
  175.7 1.7 fusion.97
  177.4 3.1 fusion.98
  183.0 2.6 fusion.96
  185.6 1.7 fusion.97
  187.3 3.1 fusion.98
  193.0 2.6 fusion.96
  195.6 1.7 fusion.97
  197.2 3.1 fusion.98
  200.7 316.2 %while.40 = (s32[]{:T(128)}, bf16[4,105,8,32]{1,3,2,0:T(8,128)(2,1)S(1)}, bf16[4,1680,512]{2,0,1:T(4,128)(2,1)}, s32[4]{0:T(128)S(1)}, bf16[4,1680,8,32]{1,3,2,0...) while((s32[]{:T(128)}, ...), condition=%wide.region_8.9_spmd, body=%wide.region_7.8_spmd.sunk | while | flops 467658240 | bytes 43092636 | solution.py:134
  203.3 3.4 exponential_divide_fusion.2
  207.2 2.2 multiply_convert_fusion.2
  209.4 2.3 fusion.109
  212.5 6.3 copy.148
  218.8 60.9 %dynamic_update_slice.29 = bf16[4,1680,512]{2,0,1:T(4,128)(2,1)} dynamic-update-slice(bf16[4,1680,512]{2,0,1:T(4,128)(2,1)} %get-tuple-element.587, bf16[1,1680,512]{2,0,1:T(2,128)(2,1)} %copy.148, s32[]{:T(128)S(6)} %copy.178, s32[]{:T(128)} %constant.35.clone.1..sunk.1, s32[]{:T(128)} %constant.35.clone.1..sunk.1) | dynamic-update-slice | bytes 3440644 | tf_op jit(solution)/shard_map/while/body/jit(dynamic_update_index_in_dim)/dynamic_update_slice | solution.py:134
  282.3 3.4 exponential_divide_fusion.2
  286.3 2.2 multiply_convert_fusion.2
  288.5 2.3 fusion.109
  291.6 6.3 copy.148
  297.9 60.9 %dynamic_update_slice.29 = bf16[4,1680,512]{2,0,1:T(4,128)(2,1)} dynamic-update-slice(bf16[4,1680,512]{2,0,1:T(4,128)(2,1)} %get-tuple-element.587, bf16[1,1680,512]{2,0,1:T(2,128)(2,1)} %copy.148, s32[]{:T(128)S(6)} %copy.178, s32[]{:T(128)} %constant.35.clone.1..sunk.1, s32[]{:T(128)} %constant.35.clone.1..sunk.1) | dynamic-update-slice | bytes 3440644 | tf_op jit(solution)/shard_map/while/body/jit(dynamic_update_index_in_dim)/dynamic_update_slice | solution.py:134
  361.4 3.4 exponential_divide_fusion.2
  365.3 2.2 multiply_convert_fusion.2
  367.5 2.3 fusion.109
  370.6 6.3 copy.148
  376.9 60.9 %dynamic_update_slice.29 = bf16[4,1680,512]{2,0,1:T(4,128)(2,1)} dynamic-update-slice(bf16[4,1680,512]{2,0,1:T(4,128)(2,1)} %get-tuple-element.587, bf16[1,1680,512]{2,0,1:T(2,128)(2,1)} %copy.148, s32[]{:T(128)S(6)} %copy.178, s32[]{:T(128)} %constant.35.clone.1..sunk.1, s32[]{:T(128)} %constant.35.clone.1..sunk.1) | dynamic-update-slice | bytes 3440644 | tf_op jit(solution)/shard_map/while/body/jit(dynamic_update_index_in_dim)/dynamic_update_slice | solution.py:134
  440.4 3.4 exponential_divide_fusion.2
  444.4 2.2 multiply_convert_fusion.2
  446.6 2.3 fusion.109
  449.7 6.3 copy.148
  456.0 60.9 %dynamic_update_slice.29 = bf16[4,1680,512]{2,0,1:T(4,128)(2,1)} dynamic-update-slice(bf16[4,1680,512]{2,0,1:T(4,128)(2,1)} %get-tuple-element.587, bf16[1,1680,512]{2,0,1:T(2,128)(2,1)} %copy.148, s32[]{:T(128)S(6)} %copy.178, s32[]{:T(128)} %constant.35.clone.1..sunk.1, s32[]{:T(128)} %constant.35.clone.1..sunk.1) | dynamic-update-slice | bytes 3440644 | tf_op jit(solution)/shard_map/while/body/jit(dynamic_update_index_in_dim)/dynamic_update_slice | solution.py:134
  522.0 332.0 %all-reduce.7.cloned.1.call-done = bf16[1680,4,512]{2,1,0:T(4,128)(2,1)} async-done(((bf16[1680,4,512]{2,1,0:T(4,128)(2,1)}), bf16[1680,4,512]{2,1,0:T(4,128)(2,1)}) %all-reduce.7.cloned.1.call-update) | async-done | bytes 6881296
  857.4 130.1 %all-reduce.11.cloned.1.call-done = (f32[256,256]{0,1:T(8,128)}, f32[256,256]{0,1:T(8,128)}, f32[256,256]{0,1:T(8,128)}, f32[256,256]{1,0:T(8,128)}) async-done(((f32[256,256]{0,1:T(8,128)}, f32[256,256]{0,1:T(8,128)}, f32[256,256]{0,1:T(8,128)}, f32[256,256]{1,0:T(8,128)}), (f32[256,256]{0,1:T(8,128)}, f32[256,256]{0,1:T(8,128)}, f32[256,256]{0,1:T(8,128)}, ...) | async-done | bytes 1048592 | tf_op jit(solution)/shard_map/psum | solution.py:153
  989.5 170.8 %all-reduce.9.cloned.1.call-done = (f32[256,256]{0,1:T(8,128)}, f32[256,256]{0,1:T(8,128)}, f32[256,256]{0,1:T(8,128)}, f32[256,256]{1,0:T(8,128)}) async-done(((f32[256,256]{0,1:T(8,128)}, f32[256,256]{0,1:T(8,128)}, f32[256,256]{0,1:T(8,128)}, f32[256,256]{1,0:T(8,128)}), (f32[256,256]{0,1:T(8,128)}, f32[256,256]{0,1:T(8,128)}, f32[256,256]{0,1:T(8,128)}, ...) | async-done | bytes 1048592 | tf_op jit(solution)/shard_map/psum | solution.py:153
  1160.4 1.8 copy.99
  1162.2 1.8 copy.100
  1164.0 1.8 copy.101
  1165.7 1.7 copy.193
  (165 shorter events, 56.7 us)
Async XLA Ops:
  7.2 5.5 copy-start
  7.2 7.0 copy-start.16
  7.2 126.7 %copy-start.18 = (bf16[256,256]{1,0:T(8,128)(2,1)S(1)}, bf16[256,256]{1,0:T(8,128)(2,1)}, u32[]{:S(2)}) copy-start(bf16[256,256]{1,0:T(8,128)(2,1)} %param.18) | copy-start | bytes 393220
  7.2 127.5 %all-gather.3.cloned.1.call-start = ((), (), s32[]{:S(2)}) async-start(), calls=%async_computation | async-start | bytes 3655680 | tf_op jit(solution)/shard_map/all_gather | solution.py:42
  8.3 126.0 %copy-start.1 = (bf16[420,256]{1,0:T(8,128)(2,1)}, bf16[420,256]{1,0:T(8,128)(2,1)S(1)}, u32[]{:S(2)}) copy-start(bf16[420,256]{1,0:T(8,128)(2,1)S(1)} %reshape.106) | copy-start | bytes 645124
  10.4 124.2 %copy-start.13 = (s32[105,1680]{1,0:T(8,128)S(1)}, s32[105,1680]{1,0:T(8,128)}, u32[]{:S(2)}) copy-start(s32[105,1680]{1,0:T(8,128)} %param.19) | copy-start | bytes 2116804
  10.5 143.3 %all-gather.5.cloned.1.call-start = ((), (), s32[]{:S(2)}) async-start(), calls=%async_computation.1 | async-start | bytes 3655680 | tf_op jit(solution)/shard_map/all_gather | solution.py:43
  12.6 841.5 %all-reduce.7.cloned.1.call-start = ((), (), s32[]{:S(2)}) async-start(), calls=%async_computation.2 | async-start | bytes 13762560
  14.5 3.1 collective-permute-start
  18.3 4.9 collective-permute-start
  23.9 5.5 collective-permute-start
  30.0 5.9 collective-permute-start
  36.5 5.9 collective-permute-start
  43.1 5.5 collective-permute-start
  49.2 5.5 collective-permute-start
  55.4 5.9 collective-permute-start
  61.9 5.9 collective-permute-start
  68.5 5.9 collective-permute-start
  75.0 6.7 collective-permute-start
  82.4 11.3 collective-permute-start
  94.4 11.4 collective-permute-start
  106.5 8.4 collective-permute-start
  115.6 7.5 collective-permute-start
  123.8 7.7 collective-permute-start
  133.1 0.6 copy-start.5
  133.1 0.7 copy-start.7
  133.1 0.7 copy-start.9
  133.1 0.8 copy-start.11
  133.9 26.7 %copy-start.3 = (f32[420,256]{1,0:T(8,128)}, f32[420,256]{1,0:T(8,128)S(1)}, u32[]{:S(2)}) copy-start(f32[420,256]{1,0:T(8,128)S(1)} %reshape.105) | copy-start | bytes 1290244
  516.9 0.9 copy-start.6
  516.9 1.0 copy-start.8
  516.9 1.0 copy-start.10
  516.9 1.1 copy-start.12
  516.9 1.2 copy-start.19
  516.9 3.3 copy-start.2
  516.9 338.4 %copy-start.17 = (bf16[105,4,256]{2,1,0:T(4,128)(2,1)S(1)}, bf16[105,4,256]{2,1,0:T(4,128)(2,1)}, u32[]{:S(2)}) copy-start(bf16[105,4,256]{2,1,0:T(4,128)(2,1)} %param.14) | copy-start | bytes 645124
  517.0 470.5 %copy-start.4 = (f32[420,256]{1,0:T(8,128)S(1)}, f32[420,256]{1,0:T(8,128)}, u32[]{:S(2)}) copy-start(f32[420,256]{1,0:T(8,128)} %copy-done.3) | copy-start | bytes 1290244
  517.0 470.4 %all-reduce.11.cloned.1.call-start = ((), (), s32[]{:S(2)}) async-start(), calls=%async_computation.4 | async-start | bytes 2097152 | tf_op jit(solution)/shard_map/psum | solution.py:153
  518.0 469.9 %copy-start.14 = (bf16[256,256]{1,0:T(8,128)(2,1)S(1)}, bf16[256,256]{1,0:T(8,128)(2,1)}, u32[]{:S(2)}) copy-start(bf16[256,256]{1,0:T(8,128)(2,1)} %param.16) | copy-start | bytes 393220
  519.5 468.6 %copy-start.15 = (bf16[256,256]{1,0:T(8,128)(2,1)S(1)}, bf16[256,256]{1,0:T(8,128)(2,1)}, u32[]{:S(2)}) copy-start(bf16[256,256]{1,0:T(8,128)(2,1)} %param.17) | copy-start | bytes 393220
  857.3 303.1 %all-reduce.9.cloned.1.call-start = ((), (), s32[]{:S(2)}) async-start(), calls=%async_computation.3 | async-start | bytes 2097152 | tf_op jit(solution)/shard_map/psum | solution.py:153
Sparse Core Ops, SparseCore 0:
  11.0 71.6 all-gather.2
  85.8 67.9 all-gather.4
  517.1 336.9 all-reduce.6
  857.6 129.7 all-reduce.10
  990.1 170.2 all-reduce.8
